TPU v7x, 128 devices: a whole 4x4x4 slice. The times are simulated.
128 devices in a mesh: nodes: 16 (over x, z), cols: 8 (over y, core).
Axes of the slice: x: 4, y: 4, z: 4, core: 2. Of those that a mesh axis runs over, the one named last changes fastest.
Arguments:
- node_feats: bfloat16 [32768, 256], P(('nodes', 'cols')), may hold values from -6 to 6
- tile_row: int32 [16, 2816], P('nodes', 'cols'), may hold values from 0 to 15, as said below
- tile_col: int32 [16, 2816], P('nodes', 'cols'), may hold values from 0 to 31
- tile_bits: int32 [16, 2816, 16, 128], P('nodes', 'cols'), may hold values from 0 to 255, as said below
- w_self: bfloat16 [256, 256], replicated, may hold values from -0.375 to 0.375
- w_neigh: bfloat16 [256, 256], replicated, may hold values from -1.5 to 1.5
- bias: float32 [256], replicated, may hold values from -3 to 3
- cotangent: bfloat16 [32768, 256], P(('nodes', 'cols')), may hold values from -6 to 6
Outputs:
- layer_out: bfloat16 [32768, 256], P(('nodes', 'cols'))
- feat_grad: bfloat16 [32768, 256], P(('nodes', 'cols'))
- self_grad: float32 [256, 256], replicated
- neigh_grad: float32 [256, 256], replicated
- bias_grad: float32 [256], replicated
Inputs may be any that keep to these rules, and one draw needn't show every extreme that they name: `tile_row`: destination row block of a tile within its nodes group; in every nodes group at least one block carries no tile. `tile_col`: source row block of a tile within its cols index; a block may carry several tiles. `tile_bits`: bit j of word (w, a) of a tile is its edge from destination row a to source column 8 w + j; bits above the eighth are zero; some destination rows have no edge in any tile.
All inputs are finite; a program needn't handle non-finite values.
Results may differ from a plain program's by a relative error of at most 0.0075.
Values may be sent and summed in bfloat16 or wider, within the bound.
No kernel may reach another device: no remote copies, remote signals or barrier semaphores. Data moves between devices by JAX's collectives and lax.ppermute only.
A program may use at most 64 MiB of HBM per device.

v0:
```python
import math
import jax
import jax.numpy as jnp
from jax import lax
from jax.sharding import PartitionSpec as P


def unpack_tiles(packed):
    shifts = jnp.arange(8, dtype=jnp.int32)
    edge_flags = jnp.right_shift(packed[:, :, None, :], shifts[None, None, :, None]) & 1
    return edge_flags.reshape(packed.shape[0], 128, 128)


def shards(node_feats, tile_row, tile_col, tile_bits, w_self, w_neigh, bias, cotangent):
    rows_dev = node_feats.shape[0]
    width_in = node_feats.shape[1]
    node_count = lax.axis_size("nodes")
    col_count = lax.axis_size("cols")
    per_dev = rows_dev // 128
    dest_count = col_count * per_dev
    source_count = node_count * per_dev
    tile_count = tile_row.shape[1]
    tile_group = math.gcd(tile_count, 32)
    group_count = tile_count // tile_group
    rows_here = tile_row[0].reshape(group_count, tile_group)
    cols_here = tile_col[0].reshape(group_count, tile_group)
    packed_here = tile_bits[0].reshape(group_count, tile_group, 16, 128)
    source = lax.all_gather(node_feats, "nodes", axis=0, tiled=True)
    source_blocks = source.reshape(source_count, 128, width_in)

    def forward_step(totals, tile_set):
        summed, degree = totals
        rows_blk, cols_blk, packed_blk = tile_set
        edge_flags = unpack_tiles(packed_blk)
        bits_blk = edge_flags.astype(jnp.bfloat16)
        picked = source_blocks[cols_blk]
        products = jnp.einsum("tba,tbf->taf", bits_blk, picked, preferred_element_type=jnp.float32)
        summed = summed.at[rows_blk].add(products)
        degree = degree.at[rows_blk].add(jnp.sum(edge_flags, axis=1).astype(jnp.float32))
        return ((summed, degree), None)

    initial = (
        jnp.zeros((dest_count, 128, width_in), jnp.float32),
        jnp.zeros((dest_count, 128), jnp.float32),
    )
    (partial_sum, degree_part), _ = lax.scan(
        forward_step, initial, (rows_here, cols_here, packed_here)
    )
    summed, degree = (
        lax.psum_scatter(
            partial_sum.reshape(dest_count * 128, width_in), "cols", scatter_dimension=0, tiled=True
        ),
        lax.psum_scatter(
            degree_part.reshape(dest_count * 128), "cols", scatter_dimension=0, tiled=True
        ),
    )
    degree = jnp.maximum(degree, 1.0)
    neigh_mean = (summed / degree[:, None]).astype(jnp.bfloat16)
    preact = (
        jnp.dot(node_feats, w_self, preferred_element_type=jnp.float32)
        + jnp.dot(neigh_mean, w_neigh, preferred_element_type=jnp.float32)
        + bias
    )
    sigmoid_pre = jax.nn.sigmoid(preact)
    layer_out = (preact * sigmoid_pre).astype(jnp.bfloat16)
    pre_grad = (
        cotangent.astype(jnp.float32) * sigmoid_pre * (1.0 + preact * (1.0 - sigmoid_pre))
    ).astype(jnp.bfloat16)
    self_term = jnp.dot(node_feats.T, pre_grad, preferred_element_type=jnp.float32)
    neigh_term = jnp.dot(neigh_mean.T, pre_grad, preferred_element_type=jnp.float32)
    bias_term = jnp.sum(pre_grad.astype(jnp.float32), axis=0)
    self_grad, neigh_grad, bias_grad = lax.psum(
        (self_term, neigh_term, bias_term), ("nodes", "cols")
    )
    mean_grad = (
        jnp.dot(pre_grad, w_neigh.T, preferred_element_type=jnp.float32) / degree[:, None]
    ).astype(jnp.bfloat16)
    dest_grad = lax.all_gather(mean_grad, "cols", axis=0, tiled=True)
    grad_blocks = dest_grad.reshape(dest_count, 128, width_in)

    def backward_step(src_grad, tile_set):
        rows_blk, cols_blk, packed_blk = tile_set
        bits_blk = unpack_tiles(packed_blk).astype(jnp.bfloat16)
        picked = grad_blocks[rows_blk]
        products = jnp.einsum("tba,taf->tbf", bits_blk, picked, preferred_element_type=jnp.float32)
        return (src_grad.at[cols_blk].add(products), None)

    src_total, _ = lax.scan(
        backward_step,
        jnp.zeros((source_count, 128, width_in), jnp.float32),
        (rows_here, cols_here, packed_here),
    )
    src_total = src_total.reshape(source_count * 128, width_in)
    src_grad = lax.psum_scatter(src_total, "nodes", scatter_dimension=0, tiled=True)
    feat_grad = (jnp.dot(pre_grad, w_self.T, preferred_element_type=jnp.float32) + src_grad).astype(
        jnp.bfloat16
    )
    return (layer_out, feat_grad, self_grad, neigh_grad, bias_grad)


def solution(mesh):
    return jax.shard_map(
        shards,
        mesh=mesh,
        in_specs=(
            P(("nodes", "cols"), None),
            P("nodes", "cols"),
            P("nodes", "cols"),
            P("nodes", "cols", None, None),
            P(),
            P(),
            P(),
            P(("nodes", "cols"), None),
        ),
        out_specs=(P(("nodes", "cols"), None), P(("nodes", "cols"), None), P(), P(), P()),
        check_vma=False,
    )
```

profile of v0, /device:TPU:0, one launch (start us, length us, event | category | flops | bytes accessed | tf_op | source)
XLA Modules:
  0.0 557.2 jit_solution(13627646105467495376)
XLA Ops:
  9.5 48.4 %all-gather.3.cloned.1.call-done = bf16[4096,256]{1,0:T(8,128)(2,1)} async-done(((bf16[256,256]{1,0:T(8,128)(2,1)}), bf16[4096,256]{1,0:T(8,128)(2,1)}) %all-gather.3.cloned.1.call-update) | async-done | bytes 2097168 | tf_op jit(solution)/shard_map/all_gather | solution.py:28
  58.1 182.1 %while.22 = (s32[]{:T(128)}, f32[16,128,256]{2,1,0:T(8,128)S(1)}, f32[16,128]{1,0:T(8,128)S(1)}, s32[11,32]{1,0:T(8,128)S(1)}, s32[11,32,16,128]{3,2,1,0:T(8,128...) while((s32[]{:T(128)}, f32[16,128,256]{2,1,0:T(8,128)S(1)}, ...), condition=%wide.region_4.5_spmd, body=%wide.region_0.4_spmd.sunk | while | flops 272635072 | bytes 24165348 | solution.py:46
  58.2 3.6 gather_fusion
  62.9 4.4 fusion.56
  67.2 6.5 %scatter_fusion = f32[16,128,256]{2,1,0:T(8,128)S(1)} fusion(f32[16,128,256]{2,1,0:T(8,128)S(1)} %get-tuple-element.232, s32[32]{0:T(128)S(1)} %get-tuple-element.213, f32[32,128,256]{2,1,0:T(8,128)} %fusion.56), kind=kCustom, calls=%fused_computation.2.clone.1 | custom fusion | flops 1048576 | bytes 12583040 | tf_op jit(solution)/shard_map/while/body/eval_jaxpr/scatter-add | solution.py:38
  74.7 3.6 gather_fusion
  79.4 4.4 fusion.56
  83.8 6.5 %scatter_fusion = f32[16,128,256]{2,1,0:T(8,128)S(1)} fusion(f32[16,128,256]{2,1,0:T(8,128)S(1)} %get-tuple-element.232, s32[32]{0:T(128)S(1)} %get-tuple-element.213, f32[32,128,256]{2,1,0:T(8,128)} %fusion.56), kind=kCustom, calls=%fused_computation.2.clone.1 | custom fusion | flops 1048576 | bytes 12583040 | tf_op jit(solution)/shard_map/while/body/eval_jaxpr/scatter-add | solution.py:38
  91.3 3.6 gather_fusion
  96.0 4.4 fusion.56
  100.4 6.5 %scatter_fusion = f32[16,128,256]{2,1,0:T(8,128)S(1)} fusion(f32[16,128,256]{2,1,0:T(8,128)S(1)} %get-tuple-element.232, s32[32]{0:T(128)S(1)} %get-tuple-element.213, f32[32,128,256]{2,1,0:T(8,128)} %fusion.56), kind=kCustom, calls=%fused_computation.2.clone.1 | custom fusion | flops 1048576 | bytes 12583040 | tf_op jit(solution)/shard_map/while/body/eval_jaxpr/scatter-add | solution.py:38
  107.9 3.6 gather_fusion
  112.5 4.4 fusion.56
  116.9 6.5 %scatter_fusion = f32[16,128,256]{2,1,0:T(8,128)S(1)} fusion(f32[16,128,256]{2,1,0:T(8,128)S(1)} %get-tuple-element.232, s32[32]{0:T(128)S(1)} %get-tuple-element.213, f32[32,128,256]{2,1,0:T(8,128)} %fusion.56), kind=kCustom, calls=%fused_computation.2.clone.1 | custom fusion | flops 1048576 | bytes 12583040 | tf_op jit(solution)/shard_map/while/body/eval_jaxpr/scatter-add | solution.py:38
  124.4 3.6 gather_fusion
  129.1 4.4 fusion.56
  133.5 6.5 %scatter_fusion = f32[16,128,256]{2,1,0:T(8,128)S(1)} fusion(f32[16,128,256]{2,1,0:T(8,128)S(1)} %get-tuple-element.232, s32[32]{0:T(128)S(1)} %get-tuple-element.213, f32[32,128,256]{2,1,0:T(8,128)} %fusion.56), kind=kCustom, calls=%fused_computation.2.clone.1 | custom fusion | flops 1048576 | bytes 12583040 | tf_op jit(solution)/shard_map/while/body/eval_jaxpr/scatter-add | solution.py:38
  141.0 3.6 gather_fusion
  145.7 4.4 fusion.56
  150.0 6.5 %scatter_fusion = f32[16,128,256]{2,1,0:T(8,128)S(1)} fusion(f32[16,128,256]{2,1,0:T(8,128)S(1)} %get-tuple-element.232, s32[32]{0:T(128)S(1)} %get-tuple-element.213, f32[32,128,256]{2,1,0:T(8,128)} %fusion.56), kind=kCustom, calls=%fused_computation.2.clone.1 | custom fusion | flops 1048576 | bytes 12583040 | tf_op jit(solution)/shard_map/while/body/eval_jaxpr/scatter-add | solution.py:38
  157.5 3.6 gather_fusion
  162.2 4.4 fusion.56
  166.6 6.5 %scatter_fusion = f32[16,128,256]{2,1,0:T(8,128)S(1)} fusion(f32[16,128,256]{2,1,0:T(8,128)S(1)} %get-tuple-element.232, s32[32]{0:T(128)S(1)} %get-tuple-element.213, f32[32,128,256]{2,1,0:T(8,128)} %fusion.56), kind=kCustom, calls=%fused_computation.2.clone.1 | custom fusion | flops 1048576 | bytes 12583040 | tf_op jit(solution)/shard_map/while/body/eval_jaxpr/scatter-add | solution.py:38
  174.1 3.6 gather_fusion
  178.7 4.4 fusion.56
  183.1 6.5 %scatter_fusion = f32[16,128,256]{2,1,0:T(8,128)S(1)} fusion(f32[16,128,256]{2,1,0:T(8,128)S(1)} %get-tuple-element.232, s32[32]{0:T(128)S(1)} %get-tuple-element.213, f32[32,128,256]{2,1,0:T(8,128)} %fusion.56), kind=kCustom, calls=%fused_computation.2.clone.1 | custom fusion | flops 1048576 | bytes 12583040 | tf_op jit(solution)/shard_map/while/body/eval_jaxpr/scatter-add | solution.py:38
  190.6 3.6 gather_fusion
  195.3 4.4 fusion.56
  199.7 6.5 %scatter_fusion = f32[16,128,256]{2,1,0:T(8,128)S(1)} fusion(f32[16,128,256]{2,1,0:T(8,128)S(1)} %get-tuple-element.232, s32[32]{0:T(128)S(1)} %get-tuple-element.213, f32[32,128,256]{2,1,0:T(8,128)} %fusion.56), kind=kCustom, calls=%fused_computation.2.clone.1 | custom fusion | flops 1048576 | bytes 12583040 | tf_op jit(solution)/shard_map/while/body/eval_jaxpr/scatter-add | solution.py:38
  207.2 3.6 gather_fusion
  211.9 4.4 fusion.56
  216.2 6.5 %scatter_fusion = f32[16,128,256]{2,1,0:T(8,128)S(1)} fusion(f32[16,128,256]{2,1,0:T(8,128)S(1)} %get-tuple-element.232, s32[32]{0:T(128)S(1)} %get-tuple-element.213, f32[32,128,256]{2,1,0:T(8,128)} %fusion.56), kind=kCustom, calls=%fused_computation.2.clone.1 | custom fusion | flops 1048576 | bytes 12583040 | tf_op jit(solution)/shard_map/while/body/eval_jaxpr/scatter-add | solution.py:38
  223.7 3.6 gather_fusion
  228.4 4.4 fusion.56
  232.8 6.5 %scatter_fusion = f32[16,128,256]{2,1,0:T(8,128)S(1)} fusion(f32[16,128,256]{2,1,0:T(8,128)S(1)} %get-tuple-element.232, s32[32]{0:T(128)S(1)} %get-tuple-element.213, f32[32,128,256]{2,1,0:T(8,128)} %fusion.56), kind=kCustom, calls=%fused_computation.2.clone.1 | custom fusion | flops 1048576 | bytes 12583040 | tf_op jit(solution)/shard_map/while/body/eval_jaxpr/scatter-add | solution.py:38
  243.1 13.7 %all-reduce = f32[2048]{0:T(1024)S(1)} all-reduce(f32[2048]{0:T(1024)S(1)} %bitcast.96), channel_id=3, replica_groups=mesh['nodes'=16,'cols'=8] {'cols'}, use_global_device_ids=true, to_apply=%region_6.7.clone | all-reduce | flops 2048 | bytes 16384
  256.9 17.8 %reduce-scatter.3.cloned.1.call-done = f32[256,256]{1,0:T(8,128)} async-done(((f32[2048,256]{1,0:T(8,128)}), f32[256,256]{1,0:T(8,128)}) %reduce-scatter.3.cloned.1.call-update) | async-done | bytes 262160 | tf_op jit(solution)/shard_map/reduce_scatter | solution.py:50
  274.7 2.6 convert_reduce_fusion
  280.3 20.2 %all-gather.5.cloned.1.call-done = bf16[2048,256]{1,0:T(8,128)(2,1)} async-done(((bf16[256,256]{1,0:T(8,128)(2,1)}), bf16[2048,256]{1,0:T(8,128)(2,1)}) %all-gather.5.cloned.1.call-update) | async-done | bytes 1048592 | tf_op jit(solution)/shard_map/all_gather | solution.py:78
  302.9 166.3 %while.23 = (s32[]{:T(128)}, f32[32,128,256]{2,1,0:T(8,128)}, s32[11,32]{1,0:T(8,128)}, s32[11,32,16,128]{3,2,1,0:T(8,128)}, s32[11,32]{1,0:T(8,128)}, /*index=5*/bf16[16,128,256]{2,1,0:T(8,128)(2,1)S(1)}, s32[]{:T(128)}) while((s32[]{:T(128)}, f32[32,128,256]{2,1,0:T(8,128)}, s32[11,32]{1,0:T(8,128)}, s32[11,32,16,128]{3,2,1,0:T(8,128)}, ...), condition=%wide.region_9.10_spmd, body=%wide.region_7.9_spmd.sunk | while | flops 271058112 | bytes 23862236 | solution.py:88
  305.4 2.7 fusion.60
  308.1 9.9 %scatter_fusion.1 = f32[32,128,256]{2,1,0:T(8,128)} fusion(f32[32,128,256]{2,1,0:T(8,128)} %get-tuple-element.255, s32[32]{0:T(128)S(1)} %get-tuple-element.221, f32[32,128,256]{2,1,0:T(8,128)} %fusion.60), kind=kCustom, calls=%fused_computation.4.clone.1 | custom fusion | flops 1048576 | bytes 12583040 | tf_op jit(solution)/shard_map/while/body/eval_jaxpr/scatter-add | solution.py:86
  320.4 2.7 fusion.60
  323.2 9.9 %scatter_fusion.1 = f32[32,128,256]{2,1,0:T(8,128)} fusion(f32[32,128,256]{2,1,0:T(8,128)} %get-tuple-element.255, s32[32]{0:T(128)S(1)} %get-tuple-element.221, f32[32,128,256]{2,1,0:T(8,128)} %fusion.60), kind=kCustom, calls=%fused_computation.4.clone.1 | custom fusion | flops 1048576 | bytes 12583040 | tf_op jit(solution)/shard_map/while/body/eval_jaxpr/scatter-add | solution.py:86
  335.5 2.7 fusion.60
  338.3 9.9 %scatter_fusion.1 = f32[32,128,256]{2,1,0:T(8,128)} fusion(f32[32,128,256]{2,1,0:T(8,128)} %get-tuple-element.255, s32[32]{0:T(128)S(1)} %get-tuple-element.221, f32[32,128,256]{2,1,0:T(8,128)} %fusion.60), kind=kCustom, calls=%fused_computation.4.clone.1 | custom fusion | flops 1048576 | bytes 12583040 | tf_op jit(solution)/shard_map/while/body/eval_jaxpr/scatter-add | solution.py:86
  350.6 2.7 fusion.60
  353.3 9.9 %scatter_fusion.1 = f32[32,128,256]{2,1,0:T(8,128)} fusion(f32[32,128,256]{2,1,0:T(8,128)} %get-tuple-element.255, s32[32]{0:T(128)S(1)} %get-tuple-element.221, f32[32,128,256]{2,1,0:T(8,128)} %fusion.60), kind=kCustom, calls=%fused_computation.4.clone.1 | custom fusion | flops 1048576 | bytes 12583040 | tf_op jit(solution)/shard_map/while/body/eval_jaxpr/scatter-add | solution.py:86
  365.7 2.7 fusion.60
  368.4 9.9 %scatter_fusion.1 = f32[32,128,256]{2,1,0:T(8,128)} fusion(f32[32,128,256]{2,1,0:T(8,128)} %get-tuple-element.255, s32[32]{0:T(128)S(1)} %get-tuple-element.221, f32[32,128,256]{2,1,0:T(8,128)} %fusion.60), kind=kCustom, calls=%fused_computation.4.clone.1 | custom fusion | flops 1048576 | bytes 12583040 | tf_op jit(solution)/shard_map/while/body/eval_jaxpr/scatter-add | solution.py:86
  380.8 2.7 fusion.60
  383.5 10.0 %scatter_fusion.1 = f32[32,128,256]{2,1,0:T(8,128)} fusion(f32[32,128,256]{2,1,0:T(8,128)} %get-tuple-element.255, s32[32]{0:T(128)S(1)} %get-tuple-element.221, f32[32,128,256]{2,1,0:T(8,128)} %fusion.60), kind=kCustom, calls=%fused_computation.4.clone.1 | custom fusion | flops 1048576 | bytes 12583040 | tf_op jit(solution)/shard_map/while/body/eval_jaxpr/scatter-add | solution.py:86
  395.9 2.7 fusion.60
  398.7 10.2 %scatter_fusion.1 = f32[32,128,256]{2,1,0:T(8,128)} fusion(f32[32,128,256]{2,1,0:T(8,128)} %get-tuple-element.255, s32[32]{0:T(128)S(1)} %get-tuple-element.221, f32[32,128,256]{2,1,0:T(8,128)} %fusion.60), kind=kCustom, calls=%fused_computation.4.clone.1 | custom fusion | flops 1048576 | bytes 12583040 | tf_op jit(solution)/shard_map/while/body/eval_jaxpr/scatter-add | solution.py:86
  411.3 2.7 fusion.60
  414.1 9.9 %scatter_fusion.1 = f32[32,128,256]{2,1,0:T(8,128)} fusion(f32[32,128,256]{2,1,0:T(8,128)} %get-tuple-element.255, s32[32]{0:T(128)S(1)} %get-tuple-element.221, f32[32,128,256]{2,1,0:T(8,128)} %fusion.60), kind=kCustom, calls=%fused_computation.4.clone.1 | custom fusion | flops 1048576 | bytes 12583040 | tf_op jit(solution)/shard_map/while/body/eval_jaxpr/scatter-add | solution.py:86
  426.4 2.7 fusion.60
  429.1 10.0 %scatter_fusion.1 = f32[32,128,256]{2,1,0:T(8,128)} fusion(f32[32,128,256]{2,1,0:T(8,128)} %get-tuple-element.255, s32[32]{0:T(128)S(1)} %get-tuple-element.221, f32[32,128,256]{2,1,0:T(8,128)} %fusion.60), kind=kCustom, calls=%fused_computation.4.clone.1 | custom fusion | flops 1048576 | bytes 12583040 | tf_op jit(solution)/shard_map/while/body/eval_jaxpr/scatter-add | solution.py:86
  441.6 2.7 fusion.60
  444.3 9.9 %scatter_fusion.1 = f32[32,128,256]{2,1,0:T(8,128)} fusion(f32[32,128,256]{2,1,0:T(8,128)} %get-tuple-element.255, s32[32]{0:T(128)S(1)} %get-tuple-element.221, f32[32,128,256]{2,1,0:T(8,128)} %fusion.60), kind=kCustom, calls=%fused_computation.4.clone.1 | custom fusion | flops 1048576 | bytes 12583040 | tf_op jit(solution)/shard_map/while/body/eval_jaxpr/scatter-add | solution.py:86
  456.7 2.7 fusion.60
  459.4 9.8 %scatter_fusion.1 = f32[32,128,256]{2,1,0:T(8,128)} fusion(f32[32,128,256]{2,1,0:T(8,128)} %get-tuple-element.255, s32[32]{0:T(128)S(1)} %get-tuple-element.221, f32[32,128,256]{2,1,0:T(8,128)} %fusion.60), kind=kCustom, calls=%fused_computation.4.clone.1 | custom fusion | flops 1048576 | bytes 12583040 | tf_op jit(solution)/shard_map/while/body/eval_jaxpr/scatter-add | solution.py:86
  469.8 66.2 %psum.23 = f32[256]{0:T(256)} all-reduce(f32[256]{0:T(256)S(1)} %copy-done.7), channel_id=1, replica_groups=mesh['nodes'=16,'cols'=8] {'nodes','cols'}, use_global_device_ids=true, to_apply=%region_14.15 | all-reduce | flops 256 | bytes 2048 | tf_op jit(solution)/shard_map/psum | solution.py:72
  537.9 9.3 %reduce-scatter.5.cloned.1.call-done = f32[256,256]{1,0:T(8,128)} async-done(((f32[4096,256]{1,0:T(8,128)}), f32[256,256]{1,0:T(8,128)}) %reduce-scatter.5.cloned.1.call-update) | async-done | bytes 262160 | tf_op jit(solution)/shard_map/reduce_scatter | solution.py:94
  (194 shorter events, 65.4 us)
Async XLA Ops:
  7.2 267.5 %copy-start = (bf16[256,256]{1,0:T(8,128)(2,1)S(1)}, bf16[256,256]{1,0:T(8,128)(2,1)}, u32[]{:S(2)}) copy-start(bf16[256,256]{1,0:T(8,128)(2,1)} %param.17) | copy-start | bytes 393220
  7.2 50.7 %all-gather.3.cloned.1.call-start = ((), (), s32[]{:S(2)}) async-start(), calls=%async_computation.2 | async-start | bytes 2228224 | tf_op jit(solution)/shard_map/all_gather | solution.py:28
  7.9 266.8 %reduce-scatter.3.cloned.1.call-start = ((), (), s32[]{:S(2)}) async-start(), calls=%async_computation.3 | async-start | bytes 2359296 | tf_op jit(solution)/shard_map/reduce_scatter | solution.py:50
  240.2 1.4 copy-start.1
  240.2 2.0 copy-start.5
  240.2 2.0 copy-start.6
  240.3 1.4 copy-start.11
  240.3 2.6 copy-start.3
  240.3 2.6 copy-start.4
  240.3 34.4 %copy-start.9 = (bf16[256,256]{1,0:T(8,128)(2,1)S(1)}, bf16[256,256]{1,0:T(8,128)(2,1)}, u32[]{:S(2)}) copy-start(bf16[256,256]{1,0:T(8,128)(2,1)} %param.19) | copy-start | bytes 393220
  240.3 34.4 %copy-start.10 = (f32[256]{0:T(256)S(1)}, f32[256]{0:T(256)}, u32[]{:S(2)}) copy-start(f32[256]{0:T(256)} %param.18) | copy-start | bytes 3076
  241.6 58.9 %all-gather.5.cloned.1.call-start = ((), (), s32[]{:S(2)}) async-start(), calls=%async_computation.4 | async-start | bytes 1179648 | tf_op jit(solution)/shard_map/all_gather | solution.py:78
  274.7 4.5 copy-start.8
  278.2 257.9 %all-reduce.4.cloned.1.call-start = ((), (), s32[]{:S(2)}) async-start(), calls=%async_computation.6 | async-start | bytes 1048576 | tf_op jit(solution)/shard_map/psum | solution.py:72
  280.2 267.0 %reduce-scatter.5.cloned.1.call-start = ((), (), s32[]{:S(2)}) async-start(), calls=%async_computation.5 | async-start | bytes 4456448 | tf_op jit(solution)/shard_map/reduce_scatter | solution.py:94
  300.5 2.4 copy-start.2
  469.2 0.7 copy-start.7
Sparse Core Ops, SparseCore 0:
  10.2 47.7 all-gather.2
  241.7 32.9 reduce-scatter.2
  278.3 22.1 all-gather.4
  305.8 144.6 all-reduce.3
  469.3 77.8 reduce-scatter.4
where the time goes:
time: 560 us; the launch traced here: 557 us
  other arithmetic  200 us (36%)
  waiting for transfers between devices  96.4 us (17%)
  matrix products  85.6 us (15%)
  blocking collectives  80 us (14%)
  local copies, waits for them, and re-layouts  79.4 us (14%)
  between operations  14.6 us (3%)
    scatter-add x11, other arithmetic, backward_step(): return (src_grad.at[cols_blk].add(products), None)  109 us
    scatter-add x11, other arithmetic, forward_step(): summed = summed.at[rows_blk].add(products)  71.1 us
    psum x1, blocking collectives, shards(): lax.psum((self_term, neigh_term, bias_term), ('nodes', 'cols'))  66.2 us
    all_gather x1, waiting for transfers between devices, shards(): source = lax.all_gather(node_feats, 'nodes', axis=0, tiled=True)  48.4 us
    dot_general x11, matrix products, forward_step(): jnp.einsum('tba,tbf->taf', bits_blk, picked, preferred_element_type=jnp.f...  48.1 us
    gather x11, local copies, waits for them, and re-layouts, forward_step(): picked = source_blocks[cols_blk]  39.8 us
    dot_general x11, matrix products, backward_step(): jnp.einsum('tba,taf->tbf', bits_blk, picked, preferred_element_type=jnp.f...  30.1 us
    shift_right_arithmetic x66, local copies, waits for them, and re-layouts, unpack_tiles(): jnp.right_shift(packed[:, :, None, :], shifts[None, None, :, None]) & 1  23.4 us
  transfers between devices with their start and end apart: 5, of which 4 were waited for; matrix products, arithmetic and copies ran while one was open for 31% of the time, Pallas kernels for 0%

commit v1 on v0

--- a/solution.py
+++ b/solution.py
@@ -70,7 +70,7 @@
     neigh_term = jnp.dot(neigh_mean.T, pre_grad, preferred_element_type=jnp.float32)
     bias_term = jnp.sum(pre_grad.astype(jnp.float32), axis=0)
     self_grad, neigh_grad, bias_grad = lax.psum(
-        (self_term, neigh_term, bias_term), ("nodes", "cols")
+        lax.psum((self_term, neigh_term, bias_term), "nodes"), "cols"
     )
     mean_grad = (
         jnp.dot(pre_grad, w_neigh.T, preferred_element_type=jnp.float32) / degree[:, None]

time: 560 us -> 648 us (1.16)
  waiting for transfers between devices: 96.4 us -> 196 us
  blocking collectives: 80 us -> 68.3 us
    psum x1 -> x2, waiting for transfers between devices: 0.01 us -> 83.3 us  [the longest x1 83.3 us: shards(): lax.psum((self_term, neigh_term, bias_term), 'nodes')]
    psum x1 -> x2, blocking collectives: 66.2 us -> 54.6 us  [the longest x1 40.9 us: shards(): lax.psum((self_term, neigh_term, bias_term), 'nodes')]
    reduce_scatter x1, waiting for transfers between devices: 9.32 us -> 20.8 us  [shards(): lax.psum_scatter(src_total, 'nodes', scatter_dimension=0, tiled=True)]
  transfers between devices with their start and end apart: 5 -> 6, of which waited for: 4 -> 5; matrix products, arithmetic and copies ran while one was open for 31% -> 27% of each run, Pallas kernels for 0% -> 0%
where the time goes in v1:
time: 648 us; the launch traced here: 645 us
  other arithmetic  200 us (31%)
  waiting for transfers between devices  196 us (30%)
  matrix products  85.6 us (13%)
  local copies, waits for them, and re-layouts  79.4 us (12%)
  blocking collectives  68.3 us (11%)
  between operations  14.9 us (2%)
    scatter-add x11, other arithmetic, backward_step(): return (src_grad.at[cols_blk].add(products), None)  109 us
    psum x1, waiting for transfers between devices, shards(): lax.psum((self_term, neigh_term, bias_term), 'nodes')  83.3 us
    scatter-add x11, other arithmetic, forward_step(): summed = summed.at[rows_blk].add(products)  71.1 us
    all_gather x1, waiting for transfers between devices, shards(): source = lax.all_gather(node_feats, 'nodes', axis=0, tiled=True)  48.4 us
    dot_general x11, matrix products, forward_step(): jnp.einsum('tba,tbf->taf', bits_blk, picked, preferred_element_type=jnp.f...  48.1 us
    psum x1, blocking collectives, shards(): lax.psum((self_term, neigh_term, bias_term), 'nodes')  40.9 us
    gather x11, local copies, waits for them, and re-layouts, forward_step(): picked = source_blocks[cols_blk]  39.8 us
    dot_general x11, matrix products, backward_step(): jnp.einsum('tba,taf->tbf', bits_blk, picked, preferred_element_type=jnp.f...  30.1 us
  transfers between devices with their start and end apart: 6, of which 5 were waited for; matrix products, arithmetic and copies ran while one was open for 27% of the time, Pallas kernels for 0%

profile of v1, /device:TPU:0, one launch (start us, length us, event | category | flops | bytes accessed | tf_op | source)
XLA Modules:
  0.0 645.3 jit_solution(16224214653045145665)
XLA Ops:
  9.5 48.4 %all-gather.3.cloned.1.call-done = bf16[4096,256]{1,0:T(8,128)(2,1)} async-done(((bf16[256,256]{1,0:T(8,128)(2,1)}), bf16[4096,256]{1,0:T(8,128)(2,1)}) %all-gather.3.cloned.1.call-update) | async-done | bytes 2097168 | tf_op jit(solution)/shard_map/all_gather | solution.py:28
  58.1 182.1 %while.22 = (s32[]{:T(128)}, f32[16,128,256]{2,1,0:T(8,128)S(1)}, f32[16,128]{1,0:T(8,128)S(1)}, s32[11,32]{1,0:T(8,128)S(1)}, s32[11,32,16,128]{3,2,1,0:T(8,128...) while((s32[]{:T(128)}, f32[16,128,256]{2,1,0:T(8,128)S(1)}, ...), condition=%wide.region_4.5_spmd, body=%wide.region_0.4_spmd.sunk | while | flops 272635072 | bytes 24165348 | solution.py:46
  58.2 3.6 gather_fusion
  62.9 4.4 fusion.56
  67.2 6.5 %scatter_fusion = f32[16,128,256]{2,1,0:T(8,128)S(1)} fusion(f32[16,128,256]{2,1,0:T(8,128)S(1)} %get-tuple-element.234, s32[32]{0:T(128)S(1)} %get-tuple-element.215, f32[32,128,256]{2,1,0:T(8,128)} %fusion.56), kind=kCustom, calls=%fused_computation.2.clone.1 | custom fusion | flops 1048576 | bytes 12583040 | tf_op jit(solution)/shard_map/while/body/eval_jaxpr/scatter-add | solution.py:38
  74.7 3.6 gather_fusion
  79.4 4.4 fusion.56
  83.8 6.5 %scatter_fusion = f32[16,128,256]{2,1,0:T(8,128)S(1)} fusion(f32[16,128,256]{2,1,0:T(8,128)S(1)} %get-tuple-element.234, s32[32]{0:T(128)S(1)} %get-tuple-element.215, f32[32,128,256]{2,1,0:T(8,128)} %fusion.56), kind=kCustom, calls=%fused_computation.2.clone.1 | custom fusion | flops 1048576 | bytes 12583040 | tf_op jit(solution)/shard_map/while/body/eval_jaxpr/scatter-add | solution.py:38
  91.3 3.6 gather_fusion
  96.0 4.4 fusion.56
  100.4 6.5 %scatter_fusion = f32[16,128,256]{2,1,0:T(8,128)S(1)} fusion(f32[16,128,256]{2,1,0:T(8,128)S(1)} %get-tuple-element.234, s32[32]{0:T(128)S(1)} %get-tuple-element.215, f32[32,128,256]{2,1,0:T(8,128)} %fusion.56), kind=kCustom, calls=%fused_computation.2.clone.1 | custom fusion | flops 1048576 | bytes 12583040 | tf_op jit(solution)/shard_map/while/body/eval_jaxpr/scatter-add | solution.py:38
  107.9 3.6 gather_fusion
  112.5 4.4 fusion.56
  116.9 6.5 %scatter_fusion = f32[16,128,256]{2,1,0:T(8,128)S(1)} fusion(f32[16,128,256]{2,1,0:T(8,128)S(1)} %get-tuple-element.234, s32[32]{0:T(128)S(1)} %get-tuple-element.215, f32[32,128,256]{2,1,0:T(8,128)} %fusion.56), kind=kCustom, calls=%fused_computation.2.clone.1 | custom fusion | flops 1048576 | bytes 12583040 | tf_op jit(solution)/shard_map/while/body/eval_jaxpr/scatter-add | solution.py:38
  124.4 3.6 gather_fusion
  129.1 4.4 fusion.56
  133.5 6.5 %scatter_fusion = f32[16,128,256]{2,1,0:T(8,128)S(1)} fusion(f32[16,128,256]{2,1,0:T(8,128)S(1)} %get-tuple-element.234, s32[32]{0:T(128)S(1)} %get-tuple-element.215, f32[32,128,256]{2,1,0:T(8,128)} %fusion.56), kind=kCustom, calls=%fused_computation.2.clone.1 | custom fusion | flops 1048576 | bytes 12583040 | tf_op jit(solution)/shard_map/while/body/eval_jaxpr/scatter-add | solution.py:38
  141.0 3.6 gather_fusion
  145.7 4.4 fusion.56
  150.0 6.5 %scatter_fusion = f32[16,128,256]{2,1,0:T(8,128)S(1)} fusion(f32[16,128,256]{2,1,0:T(8,128)S(1)} %get-tuple-element.234, s32[32]{0:T(128)S(1)} %get-tuple-element.215, f32[32,128,256]{2,1,0:T(8,128)} %fusion.56), kind=kCustom, calls=%fused_computation.2.clone.1 | custom fusion | flops 1048576 | bytes 12583040 | tf_op jit(solution)/shard_map/while/body/eval_jaxpr/scatter-add | solution.py:38
  157.5 3.6 gather_fusion
  162.2 4.4 fusion.56
  166.6 6.5 %scatter_fusion = f32[16,128,256]{2,1,0:T(8,128)S(1)} fusion(f32[16,128,256]{2,1,0:T(8,128)S(1)} %get-tuple-element.234, s32[32]{0:T(128)S(1)} %get-tuple-element.215, f32[32,128,256]{2,1,0:T(8,128)} %fusion.56), kind=kCustom, calls=%fused_computation.2.clone.1 | custom fusion | flops 1048576 | bytes 12583040 | tf_op jit(solution)/shard_map/while/body/eval_jaxpr/scatter-add | solution.py:38
  174.1 3.6 gather_fusion
  178.7 4.4 fusion.56
  183.1 6.5 %scatter_fusion = f32[16,128,256]{2,1,0:T(8,128)S(1)} fusion(f32[16,128,256]{2,1,0:T(8,128)S(1)} %get-tuple-element.234, s32[32]{0:T(128)S(1)} %get-tuple-element.215, f32[32,128,256]{2,1,0:T(8,128)} %fusion.56), kind=kCustom, calls=%fused_computation.2.clone.1 | custom fusion | flops 1048576 | bytes 12583040 | tf_op jit(solution)/shard_map/while/body/eval_jaxpr/scatter-add | solution.py:38
  190.6 3.6 gather_fusion
  195.3 4.4 fusion.56
  199.7 6.5 %scatter_fusion = f32[16,128,256]{2,1,0:T(8,128)S(1)} fusion(f32[16,128,256]{2,1,0:T(8,128)S(1)} %get-tuple-element.234, s32[32]{0:T(128)S(1)} %get-tuple-element.215, f32[32,128,256]{2,1,0:T(8,128)} %fusion.56), kind=kCustom, calls=%fused_computation.2.clone.1 | custom fusion | flops 1048576 | bytes 12583040 | tf_op jit(solution)/shard_map/while/body/eval_jaxpr/scatter-add | solution.py:38
  207.2 3.6 gather_fusion
  211.9 4.4 fusion.56
  216.2 6.5 %scatter_fusion = f32[16,128,256]{2,1,0:T(8,128)S(1)} fusion(f32[16,128,256]{2,1,0:T(8,128)S(1)} %get-tuple-element.234, s32[32]{0:T(128)S(1)} %get-tuple-element.215, f32[32,128,256]{2,1,0:T(8,128)} %fusion.56), kind=kCustom, calls=%fused_computation.2.clone.1 | custom fusion | flops 1048576 | bytes 12583040 | tf_op jit(solution)/shard_map/while/body/eval_jaxpr/scatter-add | solution.py:38
  223.7 3.6 gather_fusion
  228.4 4.4 fusion.56
  232.8 6.5 %scatter_fusion = f32[16,128,256]{2,1,0:T(8,128)S(1)} fusion(f32[16,128,256]{2,1,0:T(8,128)S(1)} %get-tuple-element.234, s32[32]{0:T(128)S(1)} %get-tuple-element.215, f32[32,128,256]{2,1,0:T(8,128)} %fusion.56), kind=kCustom, calls=%fused_computation.2.clone.1 | custom fusion | flops 1048576 | bytes 12583040 | tf_op jit(solution)/shard_map/while/body/eval_jaxpr/scatter-add | solution.py:38
  243.1 13.7 %all-reduce = f32[2048]{0:T(1024)S(1)} all-reduce(f32[2048]{0:T(1024)S(1)} %bitcast.96), channel_id=3, replica_groups=mesh['nodes'=16,'cols'=8] {'cols'}, use_global_device_ids=true, to_apply=%region_6.7.clone | all-reduce | flops 2048 | bytes 16384
  256.9 17.8 %reduce-scatter.3.cloned.1.call-done = f32[256,256]{1,0:T(8,128)} async-done(((f32[2048,256]{1,0:T(8,128)}), f32[256,256]{1,0:T(8,128)}) %reduce-scatter.3.cloned.1.call-update) | async-done | bytes 262160 | tf_op jit(solution)/shard_map/reduce_scatter | solution.py:50
  280.3 83.3 %all-reduce.6.cloned.1.call-done = (f32[256,256]{0,1:T(8,128)}, f32[256,256]{1,0:T(8,128)}) async-done(((f32[256,256]{0,1:T(8,128)}, f32[256,256]{1,0:T(8,128)}), (f32[256,256]{0,1:T(8,128)}, f32[256,256]{1,0:T(8,128)})) %all-reduce.6.cloned.1.call-update) | async-done | bytes 524304 | tf_op jit(solution)/shard_map/psum | solution.py:73
  363.6 24.9 %all-gather.5.cloned.1.call-done = bf16[2048,256]{1,0:T(8,128)(2,1)} async-done(((bf16[256,256]{1,0:T(8,128)(2,1)}), bf16[2048,256]{1,0:T(8,128)(2,1)}) %all-gather.5.cloned.1.call-update) | async-done | bytes 1048592 | tf_op jit(solution)/shard_map/all_gather | solution.py:78
  390.9 166.1 %while.23 = (s32[]{:T(128)}, f32[32,128,256]{2,1,0:T(8,128)}, s32[11,32]{1,0:T(8,128)}, s32[11,32,16,128]{3,2,1,0:T(8,128)}, s32[11,32]{1,0:T(8,128)}, /*index=5*/bf16[16,128,256]{2,1,0:T(8,128)(2,1)S(1)}, s32[]{:T(128)}) while((s32[]{:T(128)}, f32[32,128,256]{2,1,0:T(8,128)}, s32[11,32]{1,0:T(8,128)}, s32[11,32,16,128]{3,2,1,0:T(8,128)}, ...), condition=%wide.region_9.10_spmd, body=%wide.region_7.9_spmd.sunk | while | flops 271058112 | bytes 23862236 | solution.py:88
  393.4 2.7 fusion.60
  396.1 9.8 %scatter_fusion.1 = f32[32,128,256]{2,1,0:T(8,128)} fusion(f32[32,128,256]{2,1,0:T(8,128)} %get-tuple-element.257, s32[32]{0:T(128)S(1)} %get-tuple-element.223, f32[32,128,256]{2,1,0:T(8,128)} %fusion.60), kind=kCustom, calls=%fused_computation.4.clone.1 | custom fusion | flops 1048576 | bytes 12583040 | tf_op jit(solution)/shard_map/while/body/eval_jaxpr/scatter-add | solution.py:86
  408.4 2.7 fusion.60
  411.2 9.9 %scatter_fusion.1 = f32[32,128,256]{2,1,0:T(8,128)} fusion(f32[32,128,256]{2,1,0:T(8,128)} %get-tuple-element.257, s32[32]{0:T(128)S(1)} %get-tuple-element.223, f32[32,128,256]{2,1,0:T(8,128)} %fusion.60), kind=kCustom, calls=%fused_computation.4.clone.1 | custom fusion | flops 1048576 | bytes 12583040 | tf_op jit(solution)/shard_map/while/body/eval_jaxpr/scatter-add | solution.py:86
  426.3 9.9 %scatter_fusion.1 = f32[32,128,256]{2,1,0:T(8,128)} fusion(f32[32,128,256]{2,1,0:T(8,128)} %get-tuple-element.257, s32[32]{0:T(128)S(1)} %get-tuple-element.223, f32[32,128,256]{2,1,0:T(8,128)} %fusion.60), kind=kCustom, calls=%fused_computation.4.clone.1 | custom fusion | flops 1048576 | bytes 12583040 | tf_op jit(solution)/shard_map/while/body/eval_jaxpr/scatter-add | solution.py:86
  438.6 2.7 fusion.60
  441.3 9.9 %scatter_fusion.1 = f32[32,128,256]{2,1,0:T(8,128)} fusion(f32[32,128,256]{2,1,0:T(8,128)} %get-tuple-element.257, s32[32]{0:T(128)S(1)} %get-tuple-element.223, f32[32,128,256]{2,1,0:T(8,128)} %fusion.60), kind=kCustom, calls=%fused_computation.4.clone.1 | custom fusion | flops 1048576 | bytes 12583040 | tf_op jit(solution)/shard_map/while/body/eval_jaxpr/scatter-add | solution.py:86
  453.7 2.7 fusion.60
  456.4 9.9 %scatter_fusion.1 = f32[32,128,256]{2,1,0:T(8,128)} fusion(f32[32,128,256]{2,1,0:T(8,128)} %get-tuple-element.257, s32[32]{0:T(128)S(1)} %get-tuple-element.223, f32[32,128,256]{2,1,0:T(8,128)} %fusion.60), kind=kCustom, calls=%fused_computation.4.clone.1 | custom fusion | flops 1048576 | bytes 12583040 | tf_op jit(solution)/shard_map/while/body/eval_jaxpr/scatter-add | solution.py:86
  468.8 2.7 fusion.60
  471.5 10.0 %scatter_fusion.1 = f32[32,128,256]{2,1,0:T(8,128)} fusion(f32[32,128,256]{2,1,0:T(8,128)} %get-tuple-element.257, s32[32]{0:T(128)S(1)} %get-tuple-element.223, f32[32,128,256]{2,1,0:T(8,128)} %fusion.60), kind=kCustom, calls=%fused_computation.4.clone.1 | custom fusion | flops 1048576 | bytes 12583040 | tf_op jit(solution)/shard_map/while/body/eval_jaxpr/scatter-add | solution.py:86
  483.9 2.7 fusion.60
  486.7 10.1 %scatter_fusion.1 = f32[32,128,256]{2,1,0:T(8,128)} fusion(f32[32,128,256]{2,1,0:T(8,128)} %get-tuple-element.257, s32[32]{0:T(128)S(1)} %get-tuple-element.223, f32[32,128,256]{2,1,0:T(8,128)} %fusion.60), kind=kCustom, calls=%fused_computation.4.clone.1 | custom fusion | flops 1048576 | bytes 12583040 | tf_op jit(solution)/shard_map/while/body/eval_jaxpr/scatter-add | solution.py:86
  499.3 2.7 fusion.60
  502.0 9.9 %scatter_fusion.1 = f32[32,128,256]{2,1,0:T(8,128)} fusion(f32[32,128,256]{2,1,0:T(8,128)} %get-tuple-element.257, s32[32]{0:T(128)S(1)} %get-tuple-element.223, f32[32,128,256]{2,1,0:T(8,128)} %fusion.60), kind=kCustom, calls=%fused_computation.4.clone.1 | custom fusion | flops 1048576 | bytes 12583040 | tf_op jit(solution)/shard_map/while/body/eval_jaxpr/scatter-add | solution.py:86
  514.3 2.7 fusion.60
  517.1 10.0 %scatter_fusion.1 = f32[32,128,256]{2,1,0:T(8,128)} fusion(f32[32,128,256]{2,1,0:T(8,128)} %get-tuple-element.257, s32[32]{0:T(128)S(1)} %get-tuple-element.223, f32[32,128,256]{2,1,0:T(8,128)} %fusion.60), kind=kCustom, calls=%fused_computation.4.clone.1 | custom fusion | flops 1048576 | bytes 12583040 | tf_op jit(solution)/shard_map/while/body/eval_jaxpr/scatter-add | solution.py:86
  529.5 2.7 fusion.60
  532.2 9.9 %scatter_fusion.1 = f32[32,128,256]{2,1,0:T(8,128)} fusion(f32[32,128,256]{2,1,0:T(8,128)} %get-tuple-element.257, s32[32]{0:T(128)S(1)} %get-tuple-element.223, f32[32,128,256]{2,1,0:T(8,128)} %fusion.60), kind=kCustom, calls=%fused_computation.4.clone.1 | custom fusion | flops 1048576 | bytes 12583040 | tf_op jit(solution)/shard_map/while/body/eval_jaxpr/scatter-add | solution.py:86
  544.6 2.7 fusion.60
  547.3 9.8 %scatter_fusion.1 = f32[32,128,256]{2,1,0:T(8,128)} fusion(f32[32,128,256]{2,1,0:T(8,128)} %get-tuple-element.257, s32[32]{0:T(128)S(1)} %get-tuple-element.223, f32[32,128,256]{2,1,0:T(8,128)} %fusion.60), kind=kCustom, calls=%fused_computation.4.clone.1 | custom fusion | flops 1048576 | bytes 12583040 | tf_op jit(solution)/shard_map/while/body/eval_jaxpr/scatter-add | solution.py:86
  557.7 40.9 %psum.46 = f32[256]{0:T(256)S(1)} all-reduce(f32[256]{0:T(256)S(1)} %copy-done.7), channel_id=1, replica_groups=mesh['nodes'=16,'cols'=8] {'nodes'}, use_global_device_ids=true, to_apply=%region_16.17 | all-reduce | flops 256 | bytes 2048 | tf_op jit(solution)/shard_map/psum | solution.py:73
  598.6 13.8 %psum.47 = f32[256]{0:T(256)} all-reduce(f32[256]{0:T(256)S(1)} %psum.46), channel_id=1, replica_groups=mesh['nodes'=16,'cols'=8] {'cols'}, use_global_device_ids=true, to_apply=%region_17.18 | all-reduce | flops 256 | bytes 2048 | tf_op jit(solution)/shard_map/psum | solution.py:72
  614.2 20.8 %reduce-scatter.5.cloned.1.call-done = f32[256,256]{1,0:T(8,128)} async-done(((f32[4096,256]{1,0:T(8,128)}), f32[256,256]{1,0:T(8,128)}) %reduce-scatter.5.cloned.1.call-update) | async-done | bytes 262160 | tf_op jit(solution)/shard_map/reduce_scatter | solution.py:94
  (198 shorter events, 70.7 us)
Async XLA Ops:
  7.2 267.5 %copy-start = (bf16[256,256]{1,0:T(8,128)(2,1)S(1)}, bf16[256,256]{1,0:T(8,128)(2,1)}, u32[]{:S(2)}) copy-start(bf16[256,256]{1,0:T(8,128)(2,1)} %param.17) | copy-start | bytes 393220
  7.2 50.7 %all-gather.3.cloned.1.call-start = ((), (), s32[]{:S(2)}) async-start(), calls=%async_computation.2 | async-start | bytes 2228224 | tf_op jit(solution)/shard_map/all_gather | solution.py:28
  7.9 266.8 %reduce-scatter.3.cloned.1.call-start = ((), (), s32[]{:S(2)}) async-start(), calls=%async_computation.3 | async-start | bytes 2359296 | tf_op jit(solution)/shard_map/reduce_scatter | solution.py:50
  240.2 1.4 copy-start.1
  240.2 2.0 copy-start.5
  240.2 2.0 copy-start.6
  240.3 1.4 copy-start.11
  240.3 2.6 copy-start.3
  240.3 2.6 copy-start.4
  240.3 34.4 %copy-start.9 = (bf16[256,256]{1,0:T(8,128)(2,1)S(1)}, bf16[256,256]{1,0:T(8,128)(2,1)}, u32[]{:S(2)}) copy-start(bf16[256,256]{1,0:T(8,128)(2,1)} %param.19) | copy-start | bytes 393220
  240.3 34.4 %copy-start.10 = (f32[256]{0:T(256)S(1)}, f32[256]{0:T(256)}, u32[]{:S(2)}) copy-start(f32[256]{0:T(256)} %param.18) | copy-start | bytes 3076
  241.6 122.0 %all-reduce.6.cloned.1.call-start = ((), (), s32[]{:S(2)}) async-start(), calls=%async_computation.6 | async-start | bytes 1048576 | tf_op jit(solution)/shard_map/psum | solution.py:73
  274.7 3.5 copy-start.8
  279.3 109.2 %all-gather.5.cloned.1.call-start = ((), (), s32[]{:S(2)}) async-start(), calls=%async_computation.4 | async-start | bytes 1179648 | tf_op jit(solution)/shard_map/all_gather | solution.py:78
  280.2 332.1 %all-reduce.8.cloned.1.call-start = ((), (), s32[]{:S(2)}) async-start(), calls=%async_computation.7 | async-start | bytes 1048576 | tf_op jit(solution)/shard_map/psum | solution.py:72
  363.6 271.4 %reduce-scatter.5.cloned.1.call-start = ((), (), s32[]{:S(2)}) async-start(), calls=%async_computation.5 | async-start | bytes 4456448 | tf_op jit(solution)/shard_map/reduce_scatter | solution.py:94
  388.5 2.4 copy-start.2
  557.1 0.7 copy-start.7
Sparse Core Ops, SparseCore 0:
  10.2 47.7 all-gather.2
  241.7 32.9 reduce-scatter.2
  279.4 84.1 all-reduce.5
  365.8 22.6 all-gather.4
  390.9 60.7 all-reduce.7
  557.2 77.6 reduce-scatter.4
